TPU v7x, 32 devices: a whole 2x2x4 slice. The times are simulated.
32 devices in a mesh: prow: 8 (over z, y), pcol: 4 (over x, core).
Axes of the slice: x: 2, y: 2, z: 4, core: 2. Of those that a mesh axis runs over, the one named last changes fastest.
Arguments:
- matrix: float32 [2048, 2048], P('prow', 'pcol'), as said below
Outputs:
- complement: float32 [2048, 2048], P('prow', 'pcol')
- panel_columns: float32 [2048, 512], P(('prow', 'pcol'))
- pivot_values: float32 [512], replicated
Inputs may be any that keep to these rules, and one draw needn't show every extreme that they name: matrix is symmetric and positive definite, with its smallest eigenvalue above a six-hundredth of its largest diagonal entry.
All inputs are finite; a program needn't handle non-finite values.
Results may differ from a plain program's by a relative error of at most 0.00014.
Values sent between devices are 32-bit elements; how exact they have to be, the bound alone decides.
A program may use at most 128 MiB of HBM per device.

v0:
```python
import jax
import jax.numpy as jnp
from jax import lax
from jax.sharding import PartitionSpec as P

NB = 256
PANELS = 2


HIGHEST = lax.Precision.HIGHEST


def from_root(array, axis, root):
    mine = lax.axis_index(axis) == root
    return lax.psum(jnp.where(mine, array, jnp.zeros_like(array)), axis)


def factor_diagonal(diagonal):
    cholesky_factor = jnp.linalg.cholesky(diagonal)
    scaling = jnp.diagonal(cholesky_factor)
    identity = jnp.eye(diagonal.shape[0], dtype=diagonal.dtype)
    inverse = jax.scipy.linalg.solve_triangular(cholesky_factor, identity, lower=True)
    return (inverse, scaling)


def against(left_side, right_side):
    return lax.dot_general(left_side, right_side, (((1,), (1,)), ((), ())), precision=HIGHEST)


def refreshed(current, weighed, partner, finished, row_base, col_base, bounds):
    row_start, row_stop, col_start, col_stop = bounds
    section = current - against(weighed, partner)
    extent = section.shape
    global_rows = row_base + row_start + lax.broadcasted_iota(jnp.int32, extent, 0)
    global_cols = col_base + col_start + lax.broadcasted_iota(jnp.int32, extent, 1)
    retained = (global_rows >= finished) & (global_cols >= finished)
    return jnp.where(retained, section, jnp.zeros_like(section))


def on_device(matrix):
    current = matrix
    row_count, col_count = matrix.shape
    col_groups = lax.axis_size("pcol")
    row_base = lax.axis_index("prow") * row_count
    col_base = lax.axis_index("pcol") * col_count
    portion = row_count // col_groups
    column_list = []
    pivot_list = []
    for panel in range(PANELS):
        first = panel * NB
        root_row = first // row_count
        row_offset = first % row_count
        root_col = first // col_count
        col_offset = first % col_count
        row_strip = current
        received = from_root(row_strip, "prow", root_row)
        inverse, scaling = factor_diagonal(received[:, col_offset : col_offset + NB])
        projected = against(current[:, col_offset : col_offset + NB], inverse)
        factored, inverse, scaling = (
            from_root(projected * scaling, "pcol", root_col),
            from_root(inverse, "pcol", root_col),
            from_root(scaling, "pcol", root_col),
        )
        partner = (
            lax.dot_general(received, inverse, (((0,), (1,)), ((), ())), precision=HIGHEST)
            * scaling
        )
        pivot = scaling * scaling
        weighed = factored / pivot
        finished = first + NB
        bounds_list = [(0, row_count, 0, col_count)]
        joined_axis = 1
        sections = [
            refreshed(current, weighed, partner, finished, row_base, col_base, bounds)
            for bounds in bounds_list
        ]
        current = sections[0]
        column_list.append(
            lax.dynamic_slice_in_dim(factored, lax.axis_index("pcol") * portion, portion, 0)
        )
        pivot_list.append(pivot)
    return (current, jnp.concatenate(column_list, axis=1), jnp.concatenate(pivot_list))


def solution(mesh):
    in_specs = (P("prow", "pcol"),)
    out_specs = (P("prow", "pcol"), P(("prow", "pcol"), None), P())
    return jax.shard_map(
        on_device, mesh=mesh, in_specs=in_specs, out_specs=out_specs, check_vma=False
    )
```

profile of v0, /device:TPU:27, one launch (start us, length us, event | category | flops | bytes accessed | tf_op | source)
XLA Modules:
  0.0 371.6 jit_solution(5616248142023145537)
XLA Ops:
  9.4 73.2 %all-reduce.8.cloned.1.call-done = f32[256,512]{0,1:T(8,128)} async-done(((f32[256,512]{0,1:T(8,128)}), f32[256,512]{0,1:T(8,128)}) %all-reduce.8.cloned.1.call-update) | async-done | bytes 524304 | tf_op jit(solution)/shard_map/psum | solution.py:15
  83.8 11.7 %cholesky.130 = f32[128,128]{1,0:T(8,128)S(1)} custom-call(f32[128,128]{1,0:T(8,128)S(1)} %cholesky.194), custom_call_target="Cholesky" | custom-call | tf_op jit(solution)/shard_map/jit(cholesky)/cholesky | solution.py:19
  95.6 9.8 %custom-call.17 = f32[1,128,128]{1,2,0:T(8,128)S(1)} custom-call(f32[1,128,128]{2,1,0:T(8,128)S(1)} %get-tuple-element.62), custom_call_target="InvertDiagBlocksLowerTriangular" | custom-call | tf_op jit(solution)/shard_map/jit(cholesky)/cholesky | solution.py:19
  105.9 11.7 %cholesky.147 = f32[128,128]{1,0:T(8,128)S(1)} custom-call(f32[128,128]{1,0:T(8,128)S(1)} %convolution_subtract_fusion.5), custom_call_target="Cholesky" | custom-call | tf_op jit(solution)/shard_map/jit(cholesky)/cholesky | solution.py:19
  119.8 4.3 %while.4 = (s32[]{:T(128)}, f32[256,256]{1,0:T(8,128)S(1)}, s32[2,2]{1,0:T(2,128)S(1)}, f32[2,128,128]{2,1,0:T(8,128)S(1)}, s32[]{:T(128)}) while((s32[]{:T(128)}, f32[256,256]{1,0:T(8,128)S(1)}, s32[2,2]{1,0:T(2,128)S(1)}, f32[2,128,128]{2,1,0:T(8,128)S(1)}, s32[]{:T(128)}) %tuple.52), condition=%wide.while_cond, body=%wide.while_body.sunk | while | flops 2 | bytes 131181 | solution.py:22
  120.6 1.4 bitcast_dynamic-update-slice_fusion.4
  122.7 1.4 bitcast_dynamic-update-slice_fusion.4
  124.1 19.7 %custom-call.18 = f32[2,128,128]{1,2,0:T(8,128)S(1)} custom-call(f32[2,128,128]{2,1,0:T(8,128)S(1)} %get-tuple-element.19), custom_call_target="InvertDiagBlocksLowerTriangular" | custom-call | tf_op jit(solution)/shard_map/jit(_solve_triangular)/triangular_solve | solution.py:22
  144.7 2.3 gather_fusion
  149.4 7.7 %psum.58 = f32[256]{0:T(256)S(1)} all-reduce(f32[256]{0:T(256)S(1)} %broadcast_select_fusion.3), channel_id=1, replica_groups=mesh['prow'=8,'pcol'=4] {'pcol'}, use_global_device_ids=true, to_apply=%region_6.9 | all-reduce | flops 256 | bytes 2048 | tf_op jit(solution)/shard_map/psum | solution.py:15
  157.1 26.7 %all-reduce.14.cloned.1.call-done = (f32[256,256]{1,0:T(8,128)}, f32[256,256]{1,0:T(8,128)}) async-done(((f32[256,256]{1,0:T(8,128)}, f32[256,256]{1,0:T(8,128)}), (f32[256,256]{1,0:T(8,128)}, f32[256,256]{1,0:T(8,128)})) %all-reduce.14.cloned.1.call-update) | async-done | bytes 524304 | tf_op jit(solution)/shard_map/psum | solution.py:15
  183.8 1.6 convolution_multiply_fusion.1
  185.5 1.4 broadcast_select_fusion
  187.0 72.0 %all-reduce.10.cloned.1.call-done = f32[256,512]{0,1:T(8,128)} async-done(((f32[256,512]{0,1:T(8,128)}), f32[256,512]{0,1:T(8,128)}) %all-reduce.10.cloned.1.call-update) | async-done | bytes 524304 | tf_op jit(solution)/shard_map/psum | solution.py:15
  260.2 11.7 %cholesky.164 = f32[128,128]{1,0:T(8,128)S(1)} custom-call(f32[128,128]{1,0:T(8,128)S(1)} %cholesky.197), custom_call_target="Cholesky" | custom-call | tf_op jit(solution)/shard_map/jit(cholesky)/cholesky | solution.py:19
  272.0 9.8 %custom-call.19 = f32[1,128,128]{1,2,0:T(8,128)S(1)} custom-call(f32[1,128,128]{2,1,0:T(8,128)S(1)} %get-tuple-element.58), custom_call_target="InvertDiagBlocksLowerTriangular" | custom-call | tf_op jit(solution)/shard_map/jit(cholesky)/cholesky | solution.py:19
  282.3 11.7 %cholesky.181 = f32[128,128]{1,0:T(8,128)S(1)} custom-call(f32[128,128]{1,0:T(8,128)S(1)} %convolution_subtract_fusion.4), custom_call_target="Cholesky" | custom-call | tf_op jit(solution)/shard_map/jit(cholesky)/cholesky | solution.py:19
  296.6 2.6 gather_fusion.1
  299.2 4.0 %while.5 = (s32[]{:T(128)}, f32[256,256]{1,0:T(8,128)S(1)}, s32[2,2]{1,0:T(2,128)S(1)}, f32[2,128,128]{2,1,0:T(8,128)S(1)}, s32[]{:T(128)}) while((s32[]{:T(128)}, f32[256,256]{1,0:T(8,128)S(1)}, s32[2,2]{1,0:T(2,128)S(1)}, f32[2,128,128]{2,1,0:T(8,128)S(1)}, s32[]{:T(128)}) %tuple.68), condition=%wide.while_cond.clone, body=%wide.while_body.clone.sunk | while | flops 2 | bytes 131181 | solution.py:22
  299.8 1.4 bitcast_dynamic-update-slice_fusion.5
  303.2 19.7 %custom-call.20 = f32[2,128,128]{1,2,0:T(8,128)S(1)} custom-call(f32[2,128,128]{2,1,0:T(8,128)S(1)} %get-tuple-element.20), custom_call_target="InvertDiagBlocksLowerTriangular" | custom-call | tf_op jit(solution)/shard_map/jit(_solve_triangular)/triangular_solve | solution.py:22
  325.9 7.7 %psum.62 = f32[256]{0:T(256)S(1)} all-reduce(f32[256]{0:T(256)S(1)} %broadcast_select_fusion.2), channel_id=1, replica_groups=mesh['prow'=8,'pcol'=4] {'pcol'}, use_global_device_ids=true, to_apply=%region_10.13 | all-reduce | flops 256 | bytes 2048 | tf_op jit(solution)/shard_map/psum | solution.py:15
  334.2 26.2 %all-reduce.12.cloned.1.call-done = (f32[256,256]{1,0:T(8,128)}, f32[256,256]{1,0:T(8,128)}) async-done(((f32[256,256]{1,0:T(8,128)}, f32[256,256]{1,0:T(8,128)}), (f32[256,256]{1,0:T(8,128)}, f32[256,256]{1,0:T(8,128)})) %all-reduce.12.cloned.1.call-update) | async-done | bytes 524304 | tf_op jit(solution)/shard_map/psum | solution.py:15
  361.2 1.6 convolution_multiply_fusion
  (84 shorter events, 21.5 us)
Async XLA Ops:
  7.2 75.5 %all-reduce.8.cloned.1.call-start = ((), (), s32[]{:S(2)}) async-start(), calls=%async_computation | async-start | bytes 1048576 | tf_op jit(solution)/shard_map/psum | solution.py:15
  9.3 174.5 %all-reduce.14.cloned.1.call-start = ((), (), s32[]{:S(2)}) async-start(), calls=%async_computation.3 | async-start | bytes 1048576 | tf_op jit(solution)/shard_map/psum | solution.py:15
  82.6 0.9 slice-start.1
  82.6 1.1 copy-start.1
  147.1 1.1 copy-start.2
  149.3 109.7 %all-reduce.10.cloned.1.call-start = ((), (), s32[]{:S(2)}) async-start(), calls=%async_computation.1 | async-start | bytes 1048576 | tf_op jit(solution)/shard_map/psum | solution.py:15
  183.8 1.6 copy-start.3
  186.9 173.4 %all-reduce.12.cloned.1.call-start = ((), (), s32[]{:S(2)}) async-start(), calls=%async_computation.2 | async-start | bytes 1048576 | tf_op jit(solution)/shard_map/psum | solution.py:15
  259.0 0.9 slice-start
  259.0 1.1 copy-start
  361.2 1.6 copy-start.4
Sparse Core Ops, SparseCore 0:
  12.0 70.6 all-reduce.7
  149.5 34.3 all-reduce.13
  187.8 71.1 all-reduce.9
  326.0 34.3 all-reduce.11
where the time goes:
time: 375 us; the launch traced here: 372 us
  waiting for transfers between devices  198 us (53%)
  other arithmetic  112 us (30%)
  local copies, waits for them, and re-layouts  18.8 us (5%)
  between operations  16.8 us (4%)
  blocking collectives  15.4 us (4%)
  matrix products  10.4 us (3%)
    psum x4, waiting for transfers between devices, from_root(): return lax.psum(jnp.where(mine, array, jnp.zeros_like(array)), axis)  198 us
    another operation x13, other arithmetic, factor_diagonal(): cholesky_factor = jnp.linalg.cholesky(diagonal)  68.6 us
    another operation x5, other arithmetic, factor_diagonal(): jax.scipy.linalg.solve_triangular(cholesky_factor, identity, lower=True)  39.4 us
    psum x2, blocking collectives, from_root(): return lax.psum(jnp.where(mine, array, jnp.zeros_like(array)), axis)  15.4 us
    another operation x15, local copies, waits for them, and re-layouts, factor_diagonal(): jax.scipy.linalg.solve_triangular(cholesky_factor, identity, lower=True)  8.1 us
  transfers between devices with their start and end apart: 4, of which 4 were waited for; matrix products, arithmetic and copies ran while one was open for 0% of the time, Pallas kernels for 0%

commit v1 on v0

v1 whole, which is shorter than its diff:
```python
import functools

import jax
import jax.numpy as jnp
from jax import lax
from jax.experimental import pallas as pl
from jax.experimental.pallas import tpu as pltpu
from jax.sharding import PartitionSpec as P

NB = 256
PANELS = 2
BLOCK = 128
SUB = 8
CHUNKS = 4

HIGHEST = lax.Precision.HIGHEST
MESH = pl.DeviceIdType.MESH
VMEM = pltpu.VMEM


def matmul(left, right):
    return lax.dot_general(
        left, right, (((1,), (0,)), ((), ())),
        precision=HIGHEST, preferred_element_type=jnp.float32,
    )


def against(left, right):
    return lax.dot_general(
        left, right, (((1,), (1,)), ((), ())),
        precision=HIGHEST, preferred_element_type=jnp.float32,
    )


def exchange(rows, cols, chain, a_ref, col_ref, diag_ref, row_ref, *sems):
    zs, zr, ys, yr, es, er, fs, fr, rs, rr, local = sems
    r, c = lax.axis_index("prow"), lax.axis_index("pcol")
    height = a_ref.shape[0]
    piece = lax.rem(r, chain)
    other = chain - 1 - piece
    partner = r - piece + other
    step = height // CHUNKS
    has_next, has_prev = r + chain < rows, r >= chain
    even = lax.rem(c, 2) == 0
    mate = c + 1 - 2 * lax.rem(c, 2)
    has_right, has_left = even & (c + 2 < cols), even & (c >= 2)
    gets = c > 0

    barrier = pltpu.get_barrier_semaphore()

    def greet(dev):
        pl.semaphore_signal(barrier, inc=1, device_id=dev, device_id_type=MESH)

    greet((partner, c))
    greet((r, mate))
    pl.when(has_next)(lambda: greet((r + chain, c)))
    pl.when(has_prev)(lambda: greet((r - chain, c)))
    pl.when(has_right)(lambda: greet((r, c + 2)))
    pl.when(has_left)(lambda: greet((r, c - 2)))
    one = lambda flag: flag.astype(jnp.int32)
    pl.semaphore_wait(
        barrier, 2 + one(has_next) + one(has_prev) + one(has_right) + one(has_left)
    )

    def remote(ref, source, target, send, recv, dev):
        return pltpu.make_async_remote_copy(
            src_ref=source, dst_ref=ref.at[target] if target is not None else ref,
            send_sem=send, recv_sem=recv, device_id=dev, device_id_type=MESH,
        )

    def part(block, k):
        return pl.ds(pl.multiple_of(block * height + k * step, step), step)

    def z_copy(k):
        s = part(piece, k)
        return remote(col_ref, col_ref.at[s], s, zs.at[k], zr.at[k], (r + chain, c))

    def y_copy(k, block):
        s = part(block, k)
        return remote(col_ref, col_ref.at[s], s, ys.at[k], yr.at[k], (partner, c))

    def mate_copy(source, block, k, q):
        s = part(block, k)
        return remote(diag_ref, source.at[s], s, es.at[q], er.at[q], (r, c + 1))

    def right_copy(source, block, k, q):
        s = part(block, k)
        return remote(diag_ref, source.at[s], s, fs.at[q], er.at[q], (r, c + 2))

    def row_mate(source):
        return remote(row_ref, source, None, rs.at[0], rr.at[0], (r, c + 1))

    def row_right(source):
        return remote(row_ref, source, None, rs.at[1], rr.at[0], (r, c + 2))

    @pl.when(jnp.logical_not(has_prev))
    def _():
        copy = pltpu.make_async_copy(
            a_ref, col_ref.at[pl.ds(pl.multiple_of(piece * height, height), height)], local.at[0]
        )
        copy.start()
        copy.wait()

    def spread(source, block, k, q):
        pl.when(even)(lambda: mate_copy(source, block, k, q).start())
        pl.when(has_right)(lambda: right_copy(source, block, k, q).start())

    for k in range(CHUNKS):
        pl.when(has_prev)(lambda: z_copy(k).wait_recv())
        pl.when(has_next)(lambda: z_copy(k).start())
        y_copy(k, piece).start()
        pl.when(c == 0)(lambda: spread(col_ref, piece, k, k))
        if k >= 1:
            y_copy(k - 1, other).wait_recv()
            pl.when(c == 0)(lambda: spread(col_ref, other, k - 1, CHUNKS + k - 1))

        @pl.when(gets)
        def _():
            if k >= 1:
                mate_copy(diag_ref, piece, k - 1, k - 1).wait_recv()
                pl.when(even)(lambda: spread(diag_ref, piece, k - 1, k - 1))
            if k >= 2:
                q = CHUNKS + k - 2
                mate_copy(diag_ref, other, k - 2, q).wait_recv()
                pl.when(even)(lambda: spread(diag_ref, other, k - 2, q))

    k = CHUNKS - 1
    y_copy(k, other).wait_recv()

    @pl.when(c == 0)
    def _():
        spread(col_ref, other, k, CHUNKS + k)
        row_mate(a_ref).start()
        pl.when(has_right)(lambda: row_right(a_ref).start())
        copies = [
            pltpu.make_async_copy(a_ref, row_ref, local.at[1]),
            pltpu.make_async_copy(col_ref, diag_ref, local.at[2]),
        ]
        for copy in copies:
            copy.start()
        for copy in copies:
            copy.wait()

    @pl.when(gets)
    def _():
        for block, k, q in (
            (piece, CHUNKS - 1, CHUNKS - 1),
            (other, CHUNKS - 2, 2 * CHUNKS - 2),
            (other, CHUNKS - 1, 2 * CHUNKS - 1),
        ):
            mate_copy(diag_ref, block, k, q).wait_recv()
            pl.when(even)(lambda: spread(diag_ref, block, k, q))
        row_mate(row_ref).wait_recv()

        @pl.when(even)
        def _():
            row_mate(row_ref).start()
            pl.when(has_right)(lambda: row_right(row_ref).start())

    for k in range(CHUNKS):
        pl.when(has_next)(lambda: z_copy(k).wait_send())
        y_copy(k, piece).wait_send()
    for q in range(2 * CHUNKS):
        block, k = (piece, q) if q < CHUNKS else (other, q - CHUNKS)
        pl.when(even)(lambda: mate_copy(diag_ref, block, k, q).wait_send())
        pl.when(has_right)(lambda: right_copy(diag_ref, block, k, q).wait_send())
    pl.when(even)(lambda: row_mate(row_ref).wait_send())
    pl.when(has_right)(lambda: row_right(row_ref).wait_send())


def eliminate(block):
    groups = BLOCK // SUB
    shape = (SUB, BLOCK)
    lane = lax.broadcasted_iota(jnp.int32, shape, 1)
    sub = lax.broadcasted_iota(jnp.int32, shape, 0)
    zero = jnp.zeros(shape, jnp.float32)
    rows = [block[w * SUB : (w + 1) * SUB, :] for w in range(groups)]
    pivots = zero
    spread = lambda x, t: jnp.broadcast_to(x[t : t + 1, :], shape)
    for v in range(groups):
        first = v * SUB
        column = {
            w: [
                jnp.broadcast_to(rows[w][:, first + t : first + t + 1], shape)
                for t in range(SUB)
            ]
            for w in range(v, groups)
        }
        inside = (lane >= first) & (lane < first + SUB)
        identity = jnp.where(lane == sub + first, 1.0, 0.0).astype(jnp.float32)
        rows[v] = jnp.where(inside, identity, rows[v])
        for w in range(v + 1, groups):
            rows[w] = jnp.where(inside, zero, rows[w])
        for t in range(SUB):
            own = column[v]
            pivot = spread(own[t], t)
            inverse = 1.0 / pivot
            pivots = jnp.where(lane == first + t, pivot, pivots)
            entries = {u: spread(own[u], t) for u in range(t + 1, SUB)}
            pivot_row = spread(rows[v], t)
            below = jnp.where(sub > t, own[t], zero)
            for u in range(t + 1, SUB):
                own[u] = own[u] - (below * entries[u]) * inverse
            rows[v] = rows[v] - (below * pivot_row) * inverse
            for w in range(v + 1, groups):
                weight = column[w][t] * inverse
                for u in range(t + 1, SUB):
                    column[w][u] = column[w][u] - weight * entries[u]
                rows[w] = rows[w] - weight * pivot_row
        rows[v] = jnp.where(lane < first + SUB, rows[v], zero)
    return jnp.concatenate(rows, axis=0), pivots[0:1, :]


def solve(a_ref, col_ref, diag_ref, row_ref, out_ref, panel_ref, pivot_ref, work, held):
    r, c = lax.axis_index("prow"), lax.axis_index("pcol")
    depth = diag_ref.shape[0]
    height, width = a_ref.shape
    count = depth // BLOCK
    work[...] = diag_ref[...]
    for b in range(count):
        here = slice(b * BLOCK, (b + 1) * BLOCK)
        inverse, pivots = eliminate(work[here, here])
        pivot_ref[:, here] = pivots
        if b:
            left = matmul(inverse, work[here, : b * BLOCK])
            work[here, : b * BLOCK] = left
        if b + 1 < count:
            after = slice((b + 1) * BLOCK, depth)
            right = matmul(inverse, work[here, after])
            lower = against(work[after, here], inverse) / pivots
            work[after, after] = work[after, after] - matmul(lower, right)
            if b:
                work[after, : b * BLOCK] = work[after, : b * BLOCK] - matmul(lower, left)
            work[after, here] = -matmul(lower, inverse)
        work[here, here] = inverse
        if b + 1 < count:
            work[here, after] = jnp.zeros((BLOCK, depth - (b + 1) * BLOCK), jnp.float32)
    factor = against(row_ref[...], work[...])
    partner = matmul(work[...], col_ref[...])
    weighed = factor / pivot_ref[...]
    update = a_ref[...] - matmul(weighed, partner)
    grow = r * height + lax.broadcasted_iota(jnp.int32, update.shape, 0)
    gcol = c * width + lax.broadcasted_iota(jnp.int32, update.shape, 1)
    out_ref[...] = jnp.where((grow >= depth) & (gcol >= depth), update, 0.0)
    grow = r * height + lax.broadcasted_iota(jnp.int32, factor.shape, 0)
    panel = lax.broadcasted_iota(jnp.int32, factor.shape, 1) // NB
    held[...] = jnp.where(grow >= panel * NB, factor, 0.0)
    portion = panel_ref.shape[0]
    panel_ref[...] = held[pl.ds(pl.multiple_of(c * portion, portion), portion), :]


def on_device(rows, cols, matrix):
    height, width = matrix.shape
    depth = NB * PANELS
    chain = depth // height
    f32 = jnp.float32
    spec = pl.BlockSpec(memory_space=VMEM)
    dma = pltpu.SemaphoreType.DMA
    col, diag, row = pl.pallas_call(
        functools.partial(exchange, rows, cols, chain),
        out_shape=[
            jax.ShapeDtypeStruct((depth, width), f32),
            jax.ShapeDtypeStruct((depth, depth), f32),
            jax.ShapeDtypeStruct((height, depth), f32),
        ],
        in_specs=[spec],
        out_specs=[spec] * 3,
        scratch_shapes=[dma((CHUNKS,))] * 4
        + [dma((2 * CHUNKS,))] * 4
        + [dma((2,)), dma((2,)), dma((3,))],
        compiler_params=pltpu.CompilerParams(
            collective_id=0, has_side_effects=True, vmem_limit_bytes=32 * 2**20
        ),
        name="exchange",
    )(matrix)
    out, panel, pivot = pl.pallas_call(
        solve,
        out_shape=[
            jax.ShapeDtypeStruct((height, width), f32),
            jax.ShapeDtypeStruct((height // cols, depth), f32),
            jax.ShapeDtypeStruct((1, depth), f32),
        ],
        in_specs=[spec] * 4,
        out_specs=[spec] * 3,
        scratch_shapes=[VMEM((depth, depth), f32), VMEM((height, depth), f32)],
        compiler_params=pltpu.CompilerParams(vmem_limit_bytes=48 * 2**20),
        name="solve",
    )(matrix, col, diag, row)
    return out, panel, pivot.reshape(depth)


def solution(mesh):
    rows, cols = mesh.shape["prow"], mesh.shape["pcol"]
    return jax.shard_map(
        functools.partial(on_device, rows, cols),
        mesh=mesh,
        in_specs=(P("prow", "pcol"),),
        out_specs=(P("prow", "pcol"), P(("prow", "pcol"), None), P()),
        check_vma=False,
    )
```

time: 375 us -> 63.5 us (0.17)
  waiting for transfers between devices: 198 us -> 0 us
  other arithmetic: 112 us -> 0 us
  Pallas kernels: 0 us -> 61.6 us
  local copies, waits for them, and re-layouts: 18.8 us -> 1.04 us
  between operations: 16.8 us -> 0.65 us
  blocking collectives: 15.4 us -> 0 us
  matrix products: 10.4 us -> 0 us
    psum x4 -> x0, waiting for transfers between devices: 198 us -> none  [from_root(): return lax.psum(jnp.where(mine, array, jnp.zeros_like(array)), axis)]
    another operation x18 -> x0, other arithmetic: 108 us -> none  [the longest x13 68.6 us: factor_diagonal(): cholesky_factor = jnp.linalg.cholesky(diagonal)]
    pallas_call x0 -> x2, Pallas kernels: none -> 61.6 us  [the longest x1 38.7 us: on_device(): pl.pallas_call(functools.partial(exchange, rows, cols, chain), out_shape=...]
    psum x2 -> x0, blocking collectives: 15.4 us -> none  [from_root(): return lax.psum(jnp.where(mine, array, jnp.zeros_like(array)), axis)]
    another operation x19 -> x0, local copies, waits for them, and re-layouts: 8.15 us -> none  [the longest x15 8.1 us: factor_diagonal(): jax.scipy.linalg.solve_triangular(cholesky_factor, identity, lower=True)]
    dot_general x6 -> x0, matrix products: 7.71 us -> none  [the longest x4 4.49 us: against(): lax.dot_general(left_side, right_side, (((1,), (1,)), ((), ())), precisio...]
    gather x2 -> x0, local copies, waits for them, and re-layouts: 4.91 us -> none  [factor_diagonal(): scaling = jnp.diagonal(cholesky_factor)]
  transfers between devices with their start and end apart: 4 -> 0, of which waited for: 4 -> 0; matrix products, arithmetic and copies ran while one was open for 0% -> 0% of each run, Pallas kernels for 0% -> 0%
where the time goes in v1:
time: 63.5 us; the launch traced here: 63.3 us
  Pallas kernels  61.6 us (97%)
  local copies, waits for them, and re-layouts  1.04 us (2%)
  between operations  0.65 us (1%)
    pallas_call x1, Pallas kernels, on_device(): pl.pallas_call(functools.partial(exchange, rows, cols, chain), out_shape=...  38.7 us
    pallas_call x1, Pallas kernels, on_device(): pl.pallas_call(solve, out_shape=[jax.ShapeDtypeStruct((height, width), f3...  22.9 us

profile of v1, /device:TPU:27, one launch (start us, length us, event | category | flops | bytes accessed | tf_op | source)
XLA Modules:
  0.0 63.3 jit_solution(4929283780644045113)
XLA Ops:
  0.6 0.0 copy-start
  0.6 1.0 %copy-done = f32[256,512]{1,0:T(8,128)S(1)} copy-done((f32[256,512]{1,0:T(8,128)S(1)}, f32[256,512]{1,0:T(8,128)}, u32[]{:S(2)}) %copy-start) | copy-done | bytes 524312
  1.7 0.0 copy-start.1
  1.7 38.7 %exchange.1 = (f32[512,512]{1,0:T(8,128)S(1)}, f32[512,512]{1,0:T(8,128)S(1)}, f32[256,512]{1,0:T(8,128)S(1)}) custom-call(f32[256,512]{1,0:T(8,128)S(1)} %copy-done), custom_call_target="tpu_custom_call" | custom-call | tf_op jit(solution)/shard_map/exchange/pallas_call | solution.py:259
  40.4 0.0 copy-done.1
  40.4 22.9 %solve.1 = (f32[256,512]{1,0:T(8,128)}, f32[64,512]{1,0:T(8,128)}, f32[1,512]{1,0:T(1,128)}) custom-call(f32[256,512]{1,0:T(8,128)S(1)} %copy-done.1, f32[512,512]{1,0:T(8,128)S(1)} %get-tuple-element.9.col_ref, f32[512,512]{1,0:T(8,128)S(1)} %get-tuple-element.10.diag_ref, f32[256,512]{1,0:T(8,128)S(1)} %get-tuple-element.11.row_ref), custom_call_target="tpu_custom_call" | custom-call | tf_op jit(solution)/shard_map/solve/pallas_call | solution.py:276
Async XLA Ops:
  0.6 1.0 %copy-start = (f32[256,512]{1,0:T(8,128)S(1)}, f32[256,512]{1,0:T(8,128)}, u32[]{:S(2)}) copy-start(f32[256,512]{1,0:T(8,128)} %a_ref.3) | copy-start | bytes 1572868
  1.7 38.7 %copy-start.1 = (f32[256,512]{1,0:T(8,128)S(1)}, f32[256,512]{1,0:T(8,128)}, u32[]{:S(2)}) copy-start(f32[256,512]{1,0:T(8,128)} %a_ref.3) | copy-start | bytes 1572868

commit v2 on v0

v2 whole, which is shorter than its diff:
```python
import functools

import jax
import jax.numpy as jnp
from jax import lax
from jax.experimental import pallas as pl
from jax.experimental.pallas import tpu as pltpu
from jax.sharding import PartitionSpec as P

NB = 256
PANELS = 2
BLOCK = 128
SUB = 8
CHUNKS = 8
ROW_CHUNKS = 4
DIAG_SLOT = (None, 0, 4, 8)
COL_SLOT = (1, 2, 3, 5, 6, 7, 9, 10)
ROW_SLOT = (1, 3, 5, 7)
SLOTS = 4

HIGHEST = lax.Precision.HIGHEST
MESH = pl.DeviceIdType.MESH
VMEM = pltpu.VMEM


def matmul(left, right):
    return lax.dot_general(
        left, right, (((1,), (0,)), ((), ())),
        precision=HIGHEST, preferred_element_type=jnp.float32,
    )


def against(left, right):
    return lax.dot_general(
        left, right, (((1,), (1,)), ((), ())),
        precision=HIGHEST, preferred_element_type=jnp.float32,
    )


def eliminate(block, pump):
    groups = BLOCK // SUB
    shape = (SUB, BLOCK)
    lane = lax.broadcasted_iota(jnp.int32, shape, 1)
    sub = lax.broadcasted_iota(jnp.int32, shape, 0)
    zero = jnp.zeros(shape, jnp.float32)
    rest = block
    done = []
    pivots = zero
    for v in range(groups):
        if v % (groups // SLOTS) == 0:
            pump(v // (groups // SLOTS))
        first = v * SUB
        own_rows, under = rest[:SUB], rest[SUB:]
        low = under.shape[0]
        wide = lambda x, t: jnp.broadcast_to(x[:, first + t : first + t + 1], x.shape)
        own = [wide(own_rows, t) for t in range(SUB)]
        inside = (lane >= first) & (lane < first + SUB)
        identity = jnp.where(lane == sub + first, 1.0, 0.0).astype(jnp.float32)
        own_rows = jnp.where(inside, identity, own_rows)
        if low:
            column = [wide(under, t) for t in range(SUB)]
            spot = lax.broadcasted_iota(jnp.int32, under.shape, 1)
            under = jnp.where((spot >= first) & (spot < first + SUB), 0.0, under)
        for t in range(SUB):
            pivot = jnp.broadcast_to(own[t][t : t + 1], shape)
            inverse = 1.0 / pivot
            pivots = jnp.where(lane == first + t, pivot, pivots)
            entries = {u: own[u][t : t + 1] for u in range(t + 1, SUB)}
            pivot_row = own_rows[t : t + 1]
            below = jnp.where(sub > t, own[t], zero)
            for u in range(t + 1, SUB):
                own[u] = own[u] - (below * entries[u]) * inverse
            own_rows = own_rows - (below * pivot_row) * inverse
            if low:
                weight = column[t] * inverse[0:1]
                for u in range(t + 1, SUB):
                    column[u] = column[u] - weight * entries[u]
                under = under - weight * pivot_row
        done.append(jnp.where(lane < first + SUB, own_rows, zero))
        rest = under
    return jnp.concatenate(done, axis=0), pivots[0:1, :]


def window(rows, cols, chain, a_ref, out_ref, panel_ref, pivot_ref,
           col_ref, diag_ref, row_ref, work, held, partner_ref, *sems):
    ds, dr, zs, zr, ys, yr, rs, rr, local = sems
    r, c = lax.axis_index("prow"), lax.axis_index("pcol")
    height, width = a_ref.shape
    depth = diag_ref.shape[0]
    count = depth // BLOCK
    piece = lax.rem(r, chain)
    other = chain - 1 - piece
    partner = r - piece + other
    has_next, has_prev = r + chain < rows, r >= chain
    even = lax.rem(c, 2) == 0
    mate = c + 1 - 2 * lax.rem(c, 2)
    has_right, has_left = even & (c + 2 < cols), even & (c >= 2)
    lead, gets = c == 0, c > 0

    barrier = pltpu.get_barrier_semaphore()

    def greet(dev):
        pl.semaphore_signal(barrier, inc=1, device_id=dev, device_id_type=MESH)

    greet((partner, c))
    greet((r, mate))
    pl.when(has_next)(lambda: greet((r + chain, c)))
    pl.when(has_prev)(lambda: greet((r - chain, c)))
    pl.when(has_right)(lambda: greet((r, c + 2)))
    pl.when(has_left)(lambda: greet((r, c - 2)))
    one = lambda flag: flag.astype(jnp.int32)
    pl.semaphore_wait(
        barrier, 2 + one(has_next) + one(has_prev) + one(has_right) + one(has_left)
    )

    def remote(source, target, send, recv, dev):
        return pltpu.make_async_remote_copy(
            src_ref=source, dst_ref=target, send_sem=send, recv_sem=recv,
            device_id=dev, device_id_type=MESH,
        )

    def strip(b):
        return diag_ref.at[b * BLOCK : (b + 1) * BLOCK, : (b + 1) * BLOCK]

    def own_strip(b):
        top = b * BLOCK % height
        return a_ref.at[top : top + BLOCK, : (b + 1) * BLOCK]

    def strip_copy(b, way, source):
        dev = ((r + chain, c), (partner, c), (r, c + 1), (r, c + 2))[way]
        return remote(source, strip(b), ds.at[way, b], dr.at[b], dev)

    def strip_routes(b):
        mine = lead & (piece == b * BLOCK // height)
        return ((0, mine & has_next), (1, mine), (3, has_right), (2, even))

    def owner_of(b):
        return lead & (r == b * BLOCK // height)

    def local_strip(b):
        return pltpu.make_async_copy(own_strip(b), strip(b), local.at[b])

    def move_strip(b):
        owner = owner_of(b)

        @pl.when(owner)
        def _():
            for way, flag in strip_routes(b):
                pl.when(flag)(lambda: strip_copy(b, way, own_strip(b)).start())
            local_strip(b).start()
            local_strip(b).wait()

        @pl.when(jnp.logical_not(owner))
        def _():
            strip_copy(b, 2, strip(b)).wait_recv()
            for way, flag in strip_routes(b):
                pl.when(flag)(lambda: strip_copy(b, way, strip(b)).start())

    step = height // CHUNKS

    def col_part(block, k):
        start = pl.multiple_of(block * height + k * step, step)
        return col_ref.at[pl.ds(start, step)]

    def z_copy(k, source):
        return remote(source, col_part(piece, k), zs.at[k], zr.at[k], (r + chain, c))

    def y_copy(k, block, source):
        return remote(source, col_part(block, k), ys.at[k], yr.at[k], (partner, c))

    def move_col(k):
        def send(source):
            pl.when(has_next)(lambda: z_copy(k, source).start())
            y_copy(k, piece, source).start()

        @pl.when(has_prev)
        def _():
            z_copy(k, col_part(piece, k)).wait_recv()
            send(col_part(piece, k))

        pl.when(jnp.logical_not(has_prev))(
            lambda: send(a_ref.at[k * step : (k + 1) * step])
        )

    row_step = height // ROW_CHUNKS

    def row_part(ref, k):
        return ref.at[k * row_step : (k + 1) * row_step]

    def row_copy(k, way, source):
        dev = ((r, c + 1), (r, c + 2))[way]
        return remote(source, row_part(row_ref, k), rs.at[way, k], rr.at[k], dev)

    def move_row(k):
        def send(source):
            pl.when(has_right)(lambda: row_copy(k, 1, source).start())
            pl.when(even)(lambda: row_copy(k, 0, source).start())

        @pl.when(gets)
        def _():
            row_copy(k, 0, row_part(row_ref, k)).wait_recv()
            send(row_part(row_ref, k))

        pl.when(lead)(lambda: send(row_part(a_ref, k)))

    def home_col():
        start = pl.multiple_of(piece * height, height)
        return pltpu.make_async_copy(a_ref, col_ref.at[pl.ds(start, height)], local.at[count])

    def home_row():
        return pltpu.make_async_copy(a_ref, row_ref, local.at[count + 1])

    def pump(slot):
        for b in range(1, count):
            if DIAG_SLOT[b] == slot:
                move_strip(b)
        for k in range(CHUNKS):
            if COL_SLOT[k] == slot:
                move_col(k)
        for k in range(ROW_CHUNKS):
            if ROW_SLOT[k] == slot:
                move_row(k)

    move_strip(0)
    pl.when(jnp.logical_not(has_prev))(lambda: home_col().start())
    pl.when(lead)(lambda: home_row().start())
    for b in range(count):
        here = slice(b * BLOCK, (b + 1) * BLOCK)
        before = slice(0, b * BLOCK)
        current = diag_ref[here, here]
        if b:
            factor = against(diag_ref[here, before], work[before, before])
            lower = factor / pivot_ref[:, before]
            current = current - against(lower, factor)
        inverse, pivots = eliminate(current, lambda q: pump(b * SLOTS + q))
        pivot_ref[:, here] = pivots
        work[here, here] = inverse
        if b:
            work[here, before] = -matmul(inverse, matmul(lower, work[before, before]))
        if b + 1 < count:
            work[here, (b + 1) * BLOCK :] = jnp.zeros(
                (BLOCK, depth - (b + 1) * BLOCK), jnp.float32
            )

    pl.when(jnp.logical_not(has_prev))(lambda: home_col().wait())
    pl.when(lead)(lambda: home_row().wait())
    for k in range(CHUNKS):
        y_copy(k, other, col_part(other, k)).wait_recv()

    for b in range(count):
        here = slice(b * BLOCK, (b + 1) * BLOCK)
        upto = slice(0, (b + 1) * BLOCK)
        factor = against(row_ref[:, upto], work[here, upto])
        grow = r * height + lax.broadcasted_iota(jnp.int32, factor.shape, 0)
        held[:, here] = jnp.where(grow >= b * BLOCK // NB * NB, factor, 0.0)
        partner_ref[here, :] = matmul(work[here, upto], col_ref[upto, :])
    weighed = held[...] / pivot_ref[...]
    update = a_ref[...] - matmul(weighed, partner_ref[...])
    grow = r * height + lax.broadcasted_iota(jnp.int32, update.shape, 0)
    gcol = c * width + lax.broadcasted_iota(jnp.int32, update.shape, 1)
    out_ref[...] = jnp.where((grow >= depth) & (gcol >= depth), update, 0.0)
    portion = panel_ref.shape[0]
    panel_ref[...] = held[pl.ds(pl.multiple_of(c * portion, portion), portion), :]

    for b in range(count):
        for way, flag in strip_routes(b):
            pl.when(flag)(lambda: strip_copy(b, way, strip(b)).wait_send())
    for k in range(CHUNKS):
        pl.when(has_next)(lambda: z_copy(k, col_part(piece, k)).wait_send())
        y_copy(k, piece, col_part(piece, k)).wait_send()
    for k in range(ROW_CHUNKS):
        pl.when(has_right)(lambda: row_copy(k, 1, row_part(row_ref, k)).wait_send())
        pl.when(even)(lambda: row_copy(k, 0, row_part(row_ref, k)).wait_send())


def on_device(rows, cols, matrix):
    height, width = matrix.shape
    depth = NB * PANELS
    chain = depth // height
    count = depth // BLOCK
    f32 = jnp.float32
    spec = pl.BlockSpec(memory_space=VMEM)
    dma = pltpu.SemaphoreType.DMA
    out, panel, pivot = pl.pallas_call(
        functools.partial(window, rows, cols, chain),
        out_shape=[
            jax.ShapeDtypeStruct((height, width), f32),
            jax.ShapeDtypeStruct((height // cols, depth), f32),
            jax.ShapeDtypeStruct((1, depth), f32),
        ],
        in_specs=[spec],
        out_specs=[spec] * 3,
        scratch_shapes=[
            VMEM((depth, width), f32),
            VMEM((depth, depth), f32),
            VMEM((height, depth), f32),
            VMEM((depth, depth), f32),
            VMEM((height, depth), f32),
            VMEM((depth, width), f32),
            dma((4, count)),
            dma((count,)),
            dma((CHUNKS,)),
            dma((CHUNKS,)),
            dma((CHUNKS,)),
            dma((CHUNKS,)),
            dma((2, ROW_CHUNKS)),
            dma((ROW_CHUNKS,)),
            dma((count + 2,)),
        ],
        compiler_params=pltpu.CompilerParams(
            collective_id=0, has_side_effects=True, vmem_limit_bytes=48 * 2**20
        ),
        name="window",
    )(matrix)
    return out, panel, pivot.reshape(depth)


def solution(mesh):
    rows, cols = mesh.shape["prow"], mesh.shape["pcol"]
    return jax.shard_map(
        functools.partial(on_device, rows, cols),
        mesh=mesh,
        in_specs=(P("prow", "pcol"),),
        out_specs=(P("prow", "pcol"), P(("prow", "pcol"), None), P()),
        check_vma=False,
    )
```

time: 375 us -> 70.8 us (0.19)
  waiting for transfers between devices: 198 us -> 0 us
  other arithmetic: 112 us -> 0 us
  Pallas kernels: 0 us -> 66.9 us
  between operations: 16.8 us -> 0.65 us
  local copies, waits for them, and re-layouts: 18.8 us -> 3.06 us
  blocking collectives: 15.4 us -> 0 us
  matrix products: 10.4 us -> 0 us
    psum x4 -> x0, waiting for transfers between devices: 198 us -> none  [from_root(): return lax.psum(jnp.where(mine, array, jnp.zeros_like(array)), axis)]
    another operation x18 -> x0, other arithmetic: 108 us -> none  [the longest x13 68.6 us: factor_diagonal(): cholesky_factor = jnp.linalg.cholesky(diagonal)]
    pallas_call x0 -> x1, Pallas kernels: none -> 66.9 us  [on_device(): pl.pallas_call(functools.partial(window, rows, cols, chain), out_shape=[j...]
    psum x2 -> x0, blocking collectives: 15.4 us -> none  [from_root(): return lax.psum(jnp.where(mine, array, jnp.zeros_like(array)), axis)]
    another operation x19 -> x0, local copies, waits for them, and re-layouts: 8.15 us -> none  [the longest x15 8.1 us: factor_diagonal(): jax.scipy.linalg.solve_triangular(cholesky_factor, identity, lower=True)]
    dot_general x6 -> x0, matrix products: 7.71 us -> none  [the longest x4 4.49 us: against(): lax.dot_general(left_side, right_side, (((1,), (1,)), ((), ())), precisio...]
    gather x2 -> x0, local copies, waits for them, and re-layouts: 4.91 us -> none  [factor_diagonal(): scaling = jnp.diagonal(cholesky_factor)]
  transfers between devices with their start and end apart: 4 -> 0, of which waited for: 4 -> 0; matrix products, arithmetic and copies ran while one was open for 0% -> 0% of each run, Pallas kernels for 0% -> 0%
where the time goes in v2:
time: 70.8 us; the launch traced here: 70.6 us
  Pallas kernels  66.9 us (94%)
  local copies, waits for them, and re-layouts  3.06 us (4%)
    pallas_call x1, Pallas kernels, on_device(): pl.pallas_call(functools.partial(window, rows, cols, chain), out_shape=[j...  66.9 us
    unnamed x5, local copies, waits for them, and re-layouts  3.06 us

profile of v2, /device:TPU:27, one launch (start us, length us, event | category | flops | bytes accessed | tf_op | source)
XLA Modules:
  0.0 70.6 jit_solution(10078296522537677660)
XLA Ops:
  0.6 0.0 copy-start
  0.6 1.0 %copy-done = f32[256,512]{1,0:T(8,128)S(1)} copy-done((f32[256,512]{1,0:T(8,128)S(1)}, f32[256,512]{1,0:T(8,128)}, u32[]{:S(2)}) %copy-start) | copy-done | bytes 524312
  1.7 66.9 %window.1 = (f32[256,512]{1,0:T(8,128)S(1)}, f32[64,512]{1,0:T(8,128)S(1)}, f32[1,512]{1,0:T(1,128)S(1)}) custom-call(f32[256,512]{1,0:T(8,128)S(1)} %copy-done), custom_call_target="tpu_custom_call" | custom-call | tf_op jit(solution)/shard_map/window/pallas_call | solution.py:284
  68.6 0.8 %copy.7 = f32[256,512]{1,0:T(8,128)} copy(f32[256,512]{1,0:T(8,128)S(1)} %get-tuple-element.12) | data formatting | bytes 1048576
  69.4 0.7 copy.8
  70.0 0.6 copy.9
Async XLA Ops:
  0.6 1.0 %copy-start = (f32[256,512]{1,0:T(8,128)S(1)}, f32[256,512]{1,0:T(8,128)}, u32[]{:S(2)}) copy-start(f32[256,512]{1,0:T(8,128)} %a_ref.1) | copy-start | bytes 1572868

commit v3 on v1

--- a/solution.py
+++ b/solution.py
@@ -11,7 +11,8 @@
 PANELS = 2
 BLOCK = 128
 SUB = 8
-CHUNKS = 4
+CHUNKS = 8
+LAG = 3
 
 HIGHEST = lax.Precision.HIGHEST
 MESH = pl.DeviceIdType.MESH
@@ -105,6 +106,28 @@
         pl.when(even)(lambda: mate_copy(source, block, k, q).start())
         pl.when(has_right)(lambda: right_copy(source, block, k, q).start())
 
+    def take_row():
+        row_mate(row_ref).wait_recv()
+
+        @pl.when(even)
+        def _():
+            pl.when(has_right)(lambda: row_right(row_ref).start())
+            row_mate(row_ref).start()
+
+    def take(k):
+        for block, n, q in ((piece, k, k), (other, k - 1, CHUNKS + k - 1)):
+            if 0 <= n < CHUNKS:
+                mate_copy(diag_ref, block, n, q).wait_recv()
+                pl.when(even)(lambda: spread(diag_ref, block, n, q))
+
+    home = pltpu.make_async_copy(a_ref, row_ref, local.at[1])
+
+    @pl.when(c == 0)
+    def _():
+        pl.when(has_right)(lambda: row_right(a_ref).start())
+        row_mate(a_ref).start()
+        home.start()
+
     for k in range(CHUNKS):
         pl.when(has_prev)(lambda: z_copy(k).wait_recv())
         pl.when(has_next)(lambda: z_copy(k).start())
@@ -113,16 +136,10 @@
         if k >= 1:
             y_copy(k - 1, other).wait_recv()
             pl.when(c == 0)(lambda: spread(col_ref, other, k - 1, CHUNKS + k - 1))
-
-        @pl.when(gets)
-        def _():
-            if k >= 1:
-                mate_copy(diag_ref, piece, k - 1, k - 1).wait_recv()
-                pl.when(even)(lambda: spread(diag_ref, piece, k - 1, k - 1))
-            if k >= 2:
-                q = CHUNKS + k - 2
-                mate_copy(diag_ref, other, k - 2, q).wait_recv()
-                pl.when(even)(lambda: spread(diag_ref, other, k - 2, q))
+        if k == LAG:
+            pl.when(gets)(take_row)
+        if k > LAG:
+            pl.when(gets)(lambda: take(k - LAG - 1))
 
     k = CHUNKS - 1
     y_copy(k, other).wait_recv()
@@ -130,32 +147,15 @@
     @pl.when(c == 0)
     def _():
         spread(col_ref, other, k, CHUNKS + k)
-        row_mate(a_ref).start()
-        pl.when(has_right)(lambda: row_right(a_ref).start())
-        copies = [
-            pltpu.make_async_copy(a_ref, row_ref, local.at[1]),
-            pltpu.make_async_copy(col_ref, diag_ref, local.at[2]),
-        ]
-        for copy in copies:
-            copy.start()
-        for copy in copies:
-            copy.wait()
+        copy = pltpu.make_async_copy(col_ref, diag_ref, local.at[2])
+        copy.start()
+        copy.wait()
+        home.wait()
 
     @pl.when(gets)
     def _():
-        for block, k, q in (
-            (piece, CHUNKS - 1, CHUNKS - 1),
-            (other, CHUNKS - 2, 2 * CHUNKS - 2),
-            (other, CHUNKS - 1, 2 * CHUNKS - 1),
-        ):
-            mate_copy(diag_ref, block, k, q).wait_recv()
-            pl.when(even)(lambda: spread(diag_ref, block, k, q))
-        row_mate(row_ref).wait_recv()
-
-        @pl.when(even)
-        def _():
-            row_mate(row_ref).start()
-            pl.when(has_right)(lambda: row_right(row_ref).start())
+        for k in range(CHUNKS - LAG - 1, CHUNKS + 1):
+            take(k)
 
     for k in range(CHUNKS):
         pl.when(has_next)(lambda: z_copy(k).wait_send())

time: 63.5 us -> 56.3 us (0.89)
  Pallas kernels: 61.6 us -> 54.4 us
    pallas_call x1, Pallas kernels: 38.7 us -> 31.5 us  [on_device(): pl.pallas_call(functools.partial(exchange, rows, cols, chain), out_shape=...]
where the time goes in v3:
time: 56.3 us; the launch traced here: 56.1 us
  Pallas kernels  54.4 us (97%)
  local copies, waits for them, and re-layouts  1.04 us (2%)
  between operations  0.65 us (1%)
    pallas_call x1, Pallas kernels, on_device(): pl.pallas_call(functools.partial(exchange, rows, cols, chain), out_shape=...  31.5 us
    pallas_call x1, Pallas kernels, on_device(): pl.pallas_call(solve, out_shape=[jax.ShapeDtypeStruct((height, width), f3...  22.9 us

profile of v3, /device:TPU:27, one launch (start us, length us, event | category | flops | bytes accessed | tf_op | source)
XLA Modules:
  0.0 56.1 jit_solution(12947148133077109715)
XLA Ops:
  0.6 0.0 copy-start
  0.6 1.0 %copy-done = f32[256,512]{1,0:T(8,128)S(1)} copy-done((f32[256,512]{1,0:T(8,128)S(1)}, f32[256,512]{1,0:T(8,128)}, u32[]{:S(2)}) %copy-start) | copy-done | bytes 524312
  1.7 0.0 copy-start.1
  1.7 31.5 %exchange.1 = (f32[512,512]{1,0:T(8,128)S(1)}, f32[512,512]{1,0:T(8,128)S(1)}, f32[256,512]{1,0:T(8,128)S(1)}) custom-call(f32[256,512]{1,0:T(8,128)S(1)} %copy-done), custom_call_target="tpu_custom_call" | custom-call | tf_op jit(solution)/shard_map/exchange/pallas_call | solution.py:259
  33.2 0.0 copy-done.1
  33.2 22.9 %solve.1 = (f32[256,512]{1,0:T(8,128)}, f32[64,512]{1,0:T(8,128)}, f32[1,512]{1,0:T(1,128)}) custom-call(f32[256,512]{1,0:T(8,128)S(1)} %copy-done.1, f32[512,512]{1,0:T(8,128)S(1)} %get-tuple-element.9.col_ref, f32[512,512]{1,0:T(8,128)S(1)} %get-tuple-element.10.diag_ref, f32[256,512]{1,0:T(8,128)S(1)} %get-tuple-element.11.row_ref), custom_call_target="tpu_custom_call" | custom-call | tf_op jit(solution)/shard_map/solve/pallas_call | solution.py:276
Async XLA Ops:
  0.6 1.0 %copy-start = (f32[256,512]{1,0:T(8,128)S(1)}, f32[256,512]{1,0:T(8,128)}, u32[]{:S(2)}) copy-start(f32[256,512]{1,0:T(8,128)} %a_ref.3) | copy-start | bytes 1572868
  1.7 31.5 %copy-start.1 = (f32[256,512]{1,0:T(8,128)S(1)}, f32[256,512]{1,0:T(8,128)}, u32[]{:S(2)}) copy-start(f32[256,512]{1,0:T(8,128)} %a_ref.3) | copy-start | bytes 1572868
